TPU v7x, 32 devices: a whole 2x2x4 slice. The times are simulated.
32 devices in a mesh: row: 16 (over z, x, core), col: 2 (over y).
Axes of the slice: x: 2, y: 2, z: 4, core: 2. Of those that a mesh axis runs over, the one named last changes fastest.
Arguments:
- g_occupied: bfloat16 [64, 512, 512], P(('row', 'col')), may hold values from -6 to 6
- g_virtual: bfloat16 [64, 512, 512], P(('row', 'col')), may hold values from -6 to 6
- owner: int32 [64, 1], P(('row', 'col')), may hold values from 0 to 1; in each aligned block of 2 rows (0 to 1, 2 to 3, ...) at most 2 rows name the same one
- coulomb: bfloat16 [1024, 3072], P('col', 'row'), may hold values from -0.25 to 0.25
Outputs:
- screened: bfloat16 [16384, 3072], P(('row', 'col'))
Inputs may be any that keep to these rules, and one draw needn't show every extreme that they name: `owner`: among the 2 pairs of one device, no tile column is named more than twice, and some device names one twice.
All inputs are finite; a program needn't handle non-finite values.
Results may differ from a plain program's by a relative error of at most 0.015.
Values may be sent and summed in bfloat16 or wider, within the bound.
No kernel may reach another device: no remote copies, remote signals or barrier semaphores. Data moves between devices by JAX's collectives and lax.ppermute only.
A program may use at most 64 MiB of HBM per device.

v0:
```python
import jax
import jax.numpy as jnp
from jax import lax
from jax.sharding import PartitionSpec as P


def body(g_occupied, g_virtual, owner, coulomb):
    n_col = lax.axis_size("col")
    pol = g_occupied.astype(jnp.float32) * g_virtual.astype(jnp.float32)
    targets = owner[:, 0]
    columns = jnp.arange(n_col, dtype=jnp.int32)
    onehot = (targets[:, None] == columns[None, :]).astype(jnp.float32)
    contrib = jnp.einsum("sd,sij->dij", onehot, pol).astype(jnp.bfloat16)
    received = lax.all_to_all(contrib, "col", split_axis=0, concat_axis=0, tiled=True)
    tile = jnp.sum(received.astype(jnp.float32), axis=0).astype(jnp.bfloat16)
    result = jnp.dot(
        tile, lax.all_gather(coulomb, "row", axis=1, tiled=True), preferred_element_type=jnp.float32
    )
    return result.astype(jnp.bfloat16)


def solution(mesh):
    return jax.shard_map(
        body,
        mesh=mesh,
        in_specs=(
            P(("row", "col"), None, None),
            P(("row", "col"), None, None),
            P(("row", "col"), None),
            P("col", "row"),
        ),
        out_specs=P(("row", "col"), None),
        check_vma=False,
    )
```

profile of v0, /device:TPU:0, one launch (start us, length us, event | category | flops | bytes accessed | tf_op | source)
XLA Modules:
  0.0 70.0 jit_solution(15090743242697294910)
XLA Ops:
  6.5 0.0 copy-start
  6.5 0.0 all-gather.2.cloned.1.call-start
  6.5 0.7 %all-gather.2.cloned.1.call-update = ((bf16[512,192]{0,1:T(8,128)(2,1)}), bf16[512,3072]{0,1:T(8,128)(2,1)}) async-update(((), (), s32[]{:S(2)}) %all-gather.2.cloned.1.call-start, bf16[512,192]{0,1:T(8,128)(2,1)} %param.7) | async-update | bytes 3538968
  7.3 1.8 %convert_multiply_fusion = bf16[2,512,512]{2,1,0:T(8,128)(2,1)S(1)} fusion(bf16[2,512,512]{2,1,0:T(8,128)(2,1)} %param.5, bf16[2,512,512]{2,1,0:T(8,128)(2,1)} %param.4), kind=kLoop, calls=%fused_computation.2 | loop fusion | flops 2097152 | bytes 3145728 | tf_op jit(solution)/shard_map/mul | solution.py:9
  9.1 0.0 copy-done
  9.1 1.9 %fusion = bf16[2,512,512]{2,0,1:T(2,128)(2,1)S(1)} fusion(bf16[2,512,512]{2,1,0:T(8,128)(2,1)S(1)} %convert_multiply_fusion, s32[2]{0:T(128)S(1)} %bitcast.6), kind=kOutput, calls=%fused_computation.3 | convolution fusion | flops 2097156 | bytes 2097160 | tf_op jit(solution)/shard_map/sd,sij->dij/dot_general | solution.py:13
  11.0 0.2 copy.10
  11.2 17.6 %all_to_all.5 = bf16[2,512,512]{2,1,0:T(8,128)(2,1)S(1)} all-to-all(bf16[2,512,512]{2,1,0:T(8,128)(2,1)S(1)} %copy.10), channel_id=1, replica_groups=mesh['row'=16,'col'=2] {'col'}, dimensions={0} | all-to-all | bytes 2097152 | tf_op jit(solution)/shard_map/all_to_all | solution.py:14
  28.8 0.5 reduce_sum.12
  29.3 28.5 %all-gather.2.cloned.1.call-done = bf16[512,3072]{0,1:T(8,128)(2,1)} async-done(((bf16[512,192]{0,1:T(8,128)(2,1)}), bf16[512,3072]{0,1:T(8,128)(2,1)}) %all-gather.2.cloned.1.call-update) | async-done | bytes 3145744 | tf_op jit(solution)/shard_map/all_gather | solution.py:17
  57.8 5.4 %convolution_convert_fusion = bf16[512,3072]{1,0:T(8,128)(2,1)} fusion(bf16[512,512]{1,0:T(8,128)(2,1)S(1)} %reduce_sum.12, bf16[512,3072]{0,1:T(8,128)(2,1)} %all-gather.2.cloned.1.call-done), kind=kOutput, calls=%fused_computation | convolution fusion | flops 1612185600 | bytes 6815744 | tf_op jit(solution)/shard_map/dot_general | solution.py:16
Async XLA Ops:
  6.5 2.6 %copy-start = (s32[2,1]{0,1:T(1,128)S(1)}, s32[2,1]{0,1:T(1,128)}, u32[]{:S(2)}) copy-start(s32[2,1]{0,1:T(1,128)} %param.6) | copy-start | bytes 28
  6.5 51.2 %all-gather.2.cloned.1.call-start = ((), (), s32[]{:S(2)}) async-start(), calls=%async_computation.1 | async-start | bytes 3342336 | tf_op jit(solution)/shard_map/all_gather | solution.py:17
Sparse Core Ops, SparseCore 0:
  9.6 48.0 all-gather.1
where the time goes:
time: 70.2 us; the launch traced here: 70 us
  waiting for transfers between devices  29.2 us (42%)
  blocking collectives  17.6 us (25%)
  between operations  13.4 us (19%)
  matrix products  7.25 us (10%)
  other arithmetic  2.32 us (3%)
    all_gather x1, waiting for transfers between devices, body(): lax.all_gather(coulomb, 'row', axis=1, tiled=True)  28.5 us
    all_to_all x1, blocking collectives, body(): lax.all_to_all(contrib, 'col', split_axis=0, concat_axis=0, tiled=True)  17.6 us
    dot_general x1, matrix products, body(): jnp.dot(tile, lax.all_gather(coulomb, 'row', axis=1, tiled=True), preferr...  5.38 us
    dot_general x1, matrix products, body(): contrib = jnp.einsum('sd,sij->dij', onehot, pol).astype(jnp.bfloat16)  1.87 us
    mul x1, other arithmetic, body(): pol = g_occupied.astype(jnp.float32) * g_virtual.astype(jnp.float32)  1.83 us
  transfers between devices with their start and end apart: 1, of which 1 were waited for; matrix products, arithmetic and copies ran while one was open for 6% of the time, Pallas kernels for 0%

commit v1 on v0

--- a/solution.py
+++ b/solution.py
@@ -2,9 +2,30 @@
 import jax.numpy as jnp
 from jax import lax
 from jax.sharding import PartitionSpec as P
+from jax.lax import axis_index, axis_size, ppermute
 
 
 def body(g_occupied, g_virtual, owner, coulomb):
+
+    def _open_side(xx):
+        shard_axis = "row"
+        axis_len = axis_size(shard_axis)
+        buffer = [(q, (q + 1) % axis_len) for q in range(axis_len)]
+        out_arr, raw_out = ([xx], [xx])
+        crops = [(q, (q - 1) % axis_len) for q in range(axis_len)]
+        for _ in range(axis_len // 2):
+            x_new = ppermute(out_arr[-1], shard_axis, buffer)
+            out_arr.append(x_new)
+        idx = 0
+        while idx < (axis_len - 1) // 2:
+            parts_out = ppermute(raw_out[-1], shard_axis, crops)
+            raw_out.append(parts_out)
+            idx += 1
+        front = jnp.concatenate([*out_arr[::-1], *raw_out[1:]], axis=1)
+        r_now = axis_index(shard_axis)
+        passed = jnp.roll(front, (r_now - axis_len // 2) * xx.shape[1], axis=1)
+        return passed
+
     n_col = lax.axis_size("col")
     pol = g_occupied.astype(jnp.float32) * g_virtual.astype(jnp.float32)
     targets = owner[:, 0]
@@ -13,9 +34,7 @@
     contrib = jnp.einsum("sd,sij->dij", onehot, pol).astype(jnp.bfloat16)
     received = lax.all_to_all(contrib, "col", split_axis=0, concat_axis=0, tiled=True)
     tile = jnp.sum(received.astype(jnp.float32), axis=0).astype(jnp.bfloat16)
-    result = jnp.dot(
-        tile, lax.all_gather(coulomb, "row", axis=1, tiled=True), preferred_element_type=jnp.float32
-    )
+    result = jnp.dot(tile, _open_side(coulomb), preferred_element_type=jnp.float32)
     return result.astype(jnp.bfloat16)
 
 

time: 70.2 us -> 78.6 us (1.12)
  starting transfers between devices: 0.01 us -> 36.1 us
  blocking collectives: 17.6 us -> 0 us
  between operations: 13.4 us -> 0.3 us
  local copies, waits for them, and re-layouts: 0.17 us -> 7.19 us
  waiting for transfers between devices: 29.2 us -> 25.6 us
  matrix products: 7.25 us -> 6.08 us
    ppermute x0 -> x15, starting transfers between devices: none -> 32.5 us  [the longest x7 32.1 us: _open_side(): parts_out = ppermute(raw_out[-1], shard_axis, crops)]
    all_gather x1 -> x0, waiting for transfers between devices: 28.5 us -> none  [body(): lax.all_gather(coulomb, 'row', axis=1, tiled=True)]
    ppermute x0 -> x15, waiting for transfers between devices: none -> 25.6 us  [the longest x8 20.3 us: _open_side(): x_new = ppermute(out_arr[-1], shard_axis, buffer)]
    all_to_all x1 -> x0, blocking collectives: 17.6 us -> none  [body(): lax.all_to_all(contrib, 'col', split_axis=0, concat_axis=0, tiled=True)]
    unnamed x2 -> x35, local copies, waits for them, and re-layouts: 0.01 us -> 6.04 us
    all_to_all x0 -> x1, starting transfers between devices: none -> 3.58 us  [body(): lax.all_to_all(contrib, 'col', split_axis=0, concat_axis=0, tiled=True)]
    dot_general x1, matrix products: 5.38 us -> 3.53 us  [body(): jnp.dot(tile, _open_side(coulomb), preferred_element_type=jnp.float32)]
    dot_general x1, local copies, waits for them, and re-layouts: 0.17 us -> 1.14 us  [body(): contrib = jnp.einsum('sd,sij->dij', onehot, pol).astype(jnp.bfloat16)]
  transfers between devices with their start and end apart: 1 -> 16, of which waited for: 1 -> 10; matrix products, arithmetic and copies ran while one was open for 6% -> 12% of each run, Pallas kernels for 0% -> 0%
where the time goes in v1:
time: 78.6 us; the launch traced here: 78.2 us
  starting transfers between devices  36.1 us (46%)
  waiting for transfers between devices  25.6 us (33%)
  local copies, waits for them, and re-layouts  7.19 us (9%)
  matrix products  6.08 us (8%)
  other arithmetic  2.94 us (4%)
    ppermute x7, starting transfers between devices, _open_side(): parts_out = ppermute(raw_out[-1], shard_axis, crops)  32.1 us
    ppermute x8, waiting for transfers between devices, _open_side(): x_new = ppermute(out_arr[-1], shard_axis, buffer)  20.3 us
    unnamed x35, local copies, waits for them, and re-layouts  6.04 us
    ppermute x7, waiting for transfers between devices, _open_side(): parts_out = ppermute(raw_out[-1], shard_axis, crops)  5.25 us
    all_to_all x1, starting transfers between devices, body(): lax.all_to_all(contrib, 'col', split_axis=0, concat_axis=0, tiled=True)  3.58 us
    dot_general x1, matrix products, body(): jnp.dot(tile, _open_side(coulomb), preferred_element_type=jnp.float32)  3.53 us
    dot_general x1, matrix products, body(): contrib = jnp.einsum('sd,sij->dij', onehot, pol).astype(jnp.bfloat16)  2.55 us
    mul x1, other arithmetic, body(): pol = g_occupied.astype(jnp.float32) * g_virtual.astype(jnp.float32)  1.83 us
  transfers between devices with their start and end apart: 16, of which 10 were waited for; matrix products, arithmetic and copies ran while one was open for 12% of the time, Pallas kernels for 0%

profile of v1, /device:TPU:0, one launch (start us, length us, event | category | flops | bytes accessed | tf_op | source)
XLA Modules:
  0.0 78.2 jit_solution(14028791862517968533)
XLA Ops:
  0.0 0.5 collective-permute-start
  0.5 8.5 %collective-permute-done = bf16[512,192]{0,1:T(8,128)(2,1)S(1)} collective-permute-done((bf16[512,192]{0,1:T(8,128)(2,1)}, bf16[512,192]{0,1:T(8,128)(2,1)S(1)}, u32[]{:S(2)}, u32[]{:S(2)}) %collective-permute-start) | collective-permute-done | bytes 196640 | tf_op jit(solution)/shard_map/ppermute | solution.py:17
  9.0 0.0 collective-permute-start.1
  9.0 4.4 %collective-permute-start.8 = (bf16[512,192]{0,1:T(8,128)(2,1)}, bf16[512,192]{0,1:T(8,128)(2,1)S(1)}, u32[]{:S(2)}, u32[]{:S(2)}) collective-permute-start(bf16[512,192]{0,1:T(8,128)(2,1)} %param.7), channel_id=1, source_target_pairs={{0,30},{2,0},{4,2},{6,4},{8,6},{10,8},{12,10},{14,12},{16,14},{18,... | collective-permute-start | bytes 589832 | tf_op jit(solution)/shard_map/ppermute | solution.py:21
  13.4 3.3 %collective-permute-done.1 = bf16[512,192]{0,1:T(8,128)(2,1)S(1)} collective-permute-done((bf16[512,192]{0,1:T(8,128)(2,1)S(1)}, bf16[512,192]{0,1:T(8,128)(2,1)S(1)}, u32[]{:S(2)}, u32[]{:S(2)}) %collective-permute-start.1) | collective-permute-done | bytes 196640 | tf_op jit(solution)/shard_map/ppermute | solution.py:17
  16.8 0.0 collective-permute-start.2
  16.8 0.2 collective-permute-done.8
  16.9 4.6 %collective-permute-start.9 = (bf16[512,192]{0,1:T(8,128)(2,1)S(1)}, bf16[512,192]{0,1:T(8,128)(2,1)S(1)}, u32[]{:S(2)}, u32[]{:S(2)}) collective-permute-start(bf16[512,192]{0,1:T(8,128)(2,1)S(1)} %collective-permute-done.8), channel_id=1, source_target_pairs={{0,30},{2,0},{4,2},{6,4},{8,6},{10,8},{12,10},{14,12},{16,14},{18,... | collective-permute-start | bytes 589832 | tf_op jit(solution)/shard_map/ppermute | solution.py:21
  21.5 3.1 %collective-permute-done.2 = bf16[512,192]{0,1:T(8,128)(2,1)S(1)} collective-permute-done((bf16[512,192]{0,1:T(8,128)(2,1)S(1)}, bf16[512,192]{0,1:T(8,128)(2,1)S(1)}, u32[]{:S(2)}, u32[]{:S(2)}) %collective-permute-start.2) | collective-permute-done | bytes 196640 | tf_op jit(solution)/shard_map/ppermute | solution.py:17
  24.7 0.0 collective-permute-start.3
  24.7 0.0 collective-permute-done.9
  24.7 4.7 %collective-permute-start.10 = (bf16[512,192]{0,1:T(8,128)(2,1)S(1)}, bf16[512,192]{0,1:T(8,128)(2,1)S(1)}, u32[]{:S(2)}, u32[]{:S(2)}) collective-permute-start(bf16[512,192]{0,1:T(8,128)(2,1)S(1)} %collective-permute-done.9), channel_id=1, source_target_pairs={{0,30},{2,0},{4,2},{6,4},{8,6},{10,8},{12,10},{14,12},{16,14},{18,... | collective-permute-start | bytes 589832 | tf_op jit(solution)/shard_map/ppermute | solution.py:21
  29.4 3.1 %collective-permute-done.3 = bf16[512,192]{0,1:T(8,128)(2,1)S(1)} collective-permute-done((bf16[512,192]{0,1:T(8,128)(2,1)S(1)}, bf16[512,192]{0,1:T(8,128)(2,1)S(1)}, u32[]{:S(2)}, u32[]{:S(2)}) %collective-permute-start.3) | collective-permute-done | bytes 196640 | tf_op jit(solution)/shard_map/ppermute | solution.py:17
  32.6 0.0 collective-permute-start.4
  32.6 1.8 %convert_multiply_fusion = bf16[2,512,512]{2,1,0:T(8,128)(2,1)S(1)} fusion(bf16[2,512,512]{2,1,0:T(8,128)(2,1)} %param.5, bf16[2,512,512]{2,1,0:T(8,128)(2,1)} %param.4), kind=kLoop, calls=%fused_computation.3 | loop fusion | flops 2097152 | bytes 3145728 | tf_op jit(solution)/shard_map/mul | solution.py:30
  34.4 0.0 collective-permute-done.10
  34.4 4.5 %collective-permute-start.11 = (bf16[512,192]{0,1:T(8,128)(2,1)S(1)}, bf16[512,192]{0,1:T(8,128)(2,1)S(1)}, u32[]{:S(2)}, u32[]{:S(2)}) collective-permute-start(bf16[512,192]{0,1:T(8,128)(2,1)S(1)} %collective-permute-done.10), channel_id=1, source_target_pairs={{0,30},{2,0},{4,2},{6,4},{8,6},{10,8},{12,10},{14,12},{16,14},{18,... | collective-permute-start | bytes 589832 | tf_op jit(solution)/shard_map/ppermute | solution.py:21
  38.9 1.4 %collective-permute-done.4 = bf16[512,192]{0,1:T(8,128)(2,1)S(1)} collective-permute-done((bf16[512,192]{0,1:T(8,128)(2,1)S(1)}, bf16[512,192]{0,1:T(8,128)(2,1)S(1)}, u32[]{:S(2)}, u32[]{:S(2)}) %collective-permute-start.4) | collective-permute-done | bytes 196640 | tf_op jit(solution)/shard_map/ppermute | solution.py:17
  40.4 0.0 collective-permute-start.5
  40.4 0.0 copy-start
  40.4 2.6 %fusion.1 = bf16[2,512,512]{2,0,1:T(2,128)(2,1)S(1)} fusion(bf16[2,512,512]{2,1,0:T(8,128)(2,1)S(1)} %convert_multiply_fusion, s32[2]{0:T(128)} %bitcast.5), kind=kOutput, calls=%fused_computation.4 | convolution fusion | flops 2097156 | bytes 2097160 | tf_op jit(solution)/shard_map/sd,sij->dij/dot_general | solution.py:34
  42.9 1.1 %copy.10 = bf16[2,512,512]{2,1,0:T(8,128)(2,1)} copy(bf16[2,512,512]{2,0,1:T(2,128)(2,1)S(1)} %fusion.1) | data formatting | bytes 2097152 | tf_op jit(solution)/shard_map/sd,sij->dij/dot_general | solution.py:34
  44.1 3.6 %all-to-all-start = ((bf16[2,512,512]{2,1,0:T(8,128)(2,1)}), bf16[2,512,512]{2,1,0:T(8,128)(2,1)S(1)}, u32[]{:S(2)}, u32[]{:S(2)}) async-start(bf16[2,512,512]{2,1,0:T(8,128)(2,1)} %copy.10), calls=%async_computation | async-start | bytes 2097152 | tf_op jit(solution)/shard_map/all_to_all | solution.py:35
  47.7 0.0 collective-permute-done.11
  47.7 4.5 %collective-permute-start.12 = (bf16[512,192]{0,1:T(8,128)(2,1)S(1)}, bf16[512,192]{0,1:T(8,128)(2,1)S(1)}, u32[]{:S(2)}, u32[]{:S(2)}) collective-permute-start(bf16[512,192]{0,1:T(8,128)(2,1)S(1)} %collective-permute-done.11), channel_id=1, source_target_pairs={{0,30},{2,0},{4,2},{6,4},{8,6},{10,8},{12,10},{14,12},{16,14},{18,... | collective-permute-start | bytes 589832 | tf_op jit(solution)/shard_map/ppermute | solution.py:21
  52.2 0.0 collective-permute-done.5
  52.2 0.0 collective-permute-start.6
  52.2 3.2 %collective-permute-done.12 = bf16[512,192]{0,1:T(8,128)(2,1)S(1)} collective-permute-done((bf16[512,192]{0,1:T(8,128)(2,1)S(1)}, bf16[512,192]{0,1:T(8,128)(2,1)S(1)}, u32[]{:S(2)}, u32[]{:S(2)}) %collective-permute-start.12) | collective-permute-done | bytes 196640 | tf_op jit(solution)/shard_map/ppermute | solution.py:21
  55.3 4.7 %collective-permute-start.13 = (bf16[512,192]{0,1:T(8,128)(2,1)S(1)}, bf16[512,192]{0,1:T(8,128)(2,1)S(1)}, u32[]{:S(2)}, u32[]{:S(2)}) collective-permute-start(bf16[512,192]{0,1:T(8,128)(2,1)S(1)} %collective-permute-done.12), channel_id=1, source_target_pairs={{0,30},{2,0},{4,2},{6,4},{8,6},{10,8},{12,10},{14,12},{16,14},{18,... | collective-permute-start | bytes 589832 | tf_op jit(solution)/shard_map/ppermute | solution.py:21
  60.1 0.2 collective-permute-done.6
  60.3 0.0 collective-permute-start.7
  60.3 0.0 all-to-all-done
  60.3 1.1 %reduce_sum.12 = bf16[512,512]{1,0:T(8,128)(2,1)} reduce(bf16[2,512,512]{2,1,0:T(8,128)(2,1)S(1)} %all-to-all-done, bf16[]{:T(256)} %constant.25.clone.1), dimensions={0}, to_apply=%region_0.0 | reduce | flops 262144 | bytes 1572866 | tf_op jit(solution)/shard_map/reduce_sum | solution.py:36
  61.4 0.0 copy-start.1
  61.4 1.9 %collective-permute-done.13 = bf16[512,192]{0,1:T(8,128)(2,1)S(1)} collective-permute-done((bf16[512,192]{0,1:T(8,128)(2,1)S(1)}, bf16[512,192]{0,1:T(8,128)(2,1)S(1)}, u32[]{:S(2)}, u32[]{:S(2)}) %collective-permute-start.13) | collective-permute-done | bytes 196640 | tf_op jit(solution)/shard_map/ppermute | solution.py:21
  63.2 4.6 %collective-permute-start.14 = (bf16[512,192]{0,1:T(8,128)(2,1)S(1)}, bf16[512,192]{0,1:T(8,128)(2,1)S(1)}, u32[]{:S(2)}, u32[]{:S(2)}) collective-permute-start(bf16[512,192]{0,1:T(8,128)(2,1)S(1)} %collective-permute-done.13), channel_id=1, source_target_pairs={{0,30},{2,0},{4,2},{6,4},{8,6},{10,8},{12,10},{14,12},{16,14},{18,... | collective-permute-start | bytes 589832 | tf_op jit(solution)/shard_map/ppermute | solution.py:21
  67.8 0.5 collective-permute-done.7
  68.4 0.9 %constant_dynamic-update-slice_fusion.31 = bf16[512,6144]{0,1:T(8,128)(2,1)S(1)} fusion(bf16[512,192]{0,1:T(8,128)(2,1)} %collective-permute-done.7), kind=kLoop, calls=%fused_computation.37 | loop fusion | bytes 393216
  69.3 0.9 %constant_dynamic-update-slice_fusion.30 = bf16[512,6144]{0,1:T(8,128)(2,1)S(1)} fusion(bf16[512,6144]{0,1:T(8,128)(2,1)S(1)} %constant_dynamic-update-slice_fusion.31, bf16[512,192]{0,1:T(8,128)(2,1)} %collective-permute-done.6), kind=kLoop, calls=%fused_computation.36 | loop fusion | bytes 393216
  70.3 0.9 %constant_dynamic-update-slice_fusion.29 = bf16[512,6144]{0,1:T(8,128)(2,1)S(1)} fusion(bf16[512,6144]{0,1:T(8,128)(2,1)S(1)} %constant_dynamic-update-slice_fusion.30, bf16[512,192]{0,1:T(8,128)(2,1)} %collective-permute-done.5), kind=kLoop, calls=%fused_computation.35 | loop fusion | bytes 393216
  71.3 0.0 copy-done
  71.5 0.0 collective-permute-done.14
  71.5 0.9 %constant_dynamic-update-slice_fusion.15 = bf16[512,6144]{0,1:T(8,128)(2,1)S(1)} fusion(bf16[512,6144]{0,1:T(8,128)(2,1)S(1)} %constant_dynamic-update-slice_fusion.16, bf16[512,192]{0,1:T(8,128)(2,1)} %collective-permute-done.7), kind=kLoop, calls=%fused_computation.21 | loop fusion | bytes 393216
  72.5 0.9 %constant_dynamic-update-slice_fusion.14 = bf16[512,6144]{0,1:T(8,128)(2,1)S(1)} fusion(bf16[512,6144]{0,1:T(8,128)(2,1)S(1)} %constant_dynamic-update-slice_fusion.15, bf16[512,192]{0,1:T(8,128)(2,1)} %collective-permute-done.6), kind=kLoop, calls=%fused_computation.20 | loop fusion | bytes 393216
  73.4 0.9 %constant_dynamic-update-slice_fusion.13 = bf16[512,6144]{0,1:T(8,128)(2,1)S(1)} fusion(bf16[512,6144]{0,1:T(8,128)(2,1)S(1)} %constant_dynamic-update-slice_fusion.14, bf16[512,192]{0,1:T(8,128)(2,1)} %collective-permute-done.5), kind=kLoop, calls=%fused_computation.19 | loop fusion | bytes 393216
  74.7 0.0 copy-done.1
  74.7 3.5 %convolution_convert_fusion = bf16[512,3072]{1,0:T(8,128)(2,1)} fusion(bf16[512,512]{1,0:T(8,128)(2,1)S(1)} %copy-done.1, bf16[512,6144]{0,1:T(8,128)(2,1)S(1)} %constant_dynamic-update-slice_fusion, s32[]{:T(128)S(6)} %select_n.14), kind=kOutput, calls=%fused_computation | convolution fusion | flops 1612185600 | bytes 6815748 | tf_op jit(solution)/shard_map/dot_general | solution.py:37
  (26 shorter events, 0.4 us)
Async XLA Ops:
  0.0 9.0 %collective-permute-start = (bf16[512,192]{0,1:T(8,128)(2,1)}, bf16[512,192]{0,1:T(8,128)(2,1)S(1)}, u32[]{:S(2)}, u32[]{:S(2)}) collective-permute-start(bf16[512,192]{0,1:T(8,128)(2,1)} %param.7), channel_id=1, source_target_pairs={{0,2},{2,4},{4,6},{6,8},{8,10},{10,12},{12,14},{14,16},{16,18},{18... | collective-permute-start | bytes 589832 | tf_op jit(solution)/shard_map/ppermute | solution.py:17
  9.0 7.8 %collective-permute-start.1 = (bf16[512,192]{0,1:T(8,128)(2,1)S(1)}, bf16[512,192]{0,1:T(8,128)(2,1)S(1)}, u32[]{:S(2)}, u32[]{:S(2)}) collective-permute-start(bf16[512,192]{0,1:T(8,128)(2,1)S(1)} %collective-permute-done), channel_id=1, source_target_pairs={{0,2},{2,4},{4,6},{6,8},{8,10},{10,12},{12,14},{14,16},{16,18},{18... | collective-permute-start | bytes 589832 | tf_op jit(solution)/shard_map/ppermute | solution.py:17
  9.0 7.9 %collective-permute-start.8 = (bf16[512,192]{0,1:T(8,128)(2,1)}, bf16[512,192]{0,1:T(8,128)(2,1)S(1)}, u32[]{:S(2)}, u32[]{:S(2)}) collective-permute-start(bf16[512,192]{0,1:T(8,128)(2,1)} %param.7), channel_id=1, source_target_pairs={{0,30},{2,0},{4,2},{6,4},{8,6},{10,8},{12,10},{14,12},{16,14},{18,... | collective-permute-start | bytes 589832 | tf_op jit(solution)/shard_map/ppermute | solution.py:21
  16.8 7.9 %collective-permute-start.2 = (bf16[512,192]{0,1:T(8,128)(2,1)S(1)}, bf16[512,192]{0,1:T(8,128)(2,1)S(1)}, u32[]{:S(2)}, u32[]{:S(2)}) collective-permute-start(bf16[512,192]{0,1:T(8,128)(2,1)S(1)} %collective-permute-done.1), channel_id=1, source_target_pairs={{0,2},{2,4},{4,6},{6,8},{8,10},{10,12},{12,14},{14,16},{16,18},{18... | collective-permute-start | bytes 589832 | tf_op jit(solution)/shard_map/ppermute | solution.py:17
  16.9 7.8 %collective-permute-start.9 = (bf16[512,192]{0,1:T(8,128)(2,1)S(1)}, bf16[512,192]{0,1:T(8,128)(2,1)S(1)}, u32[]{:S(2)}, u32[]{:S(2)}) collective-permute-start(bf16[512,192]{0,1:T(8,128)(2,1)S(1)} %collective-permute-done.8), channel_id=1, source_target_pairs={{0,30},{2,0},{4,2},{6,4},{8,6},{10,8},{12,10},{14,12},{16,14},{18,... | collective-permute-start | bytes 589832 | tf_op jit(solution)/shard_map/ppermute | solution.py:21
  24.7 7.9 %collective-permute-start.3 = (bf16[512,192]{0,1:T(8,128)(2,1)S(1)}, bf16[512,192]{0,1:T(8,128)(2,1)S(1)}, u32[]{:S(2)}, u32[]{:S(2)}) collective-permute-start(bf16[512,192]{0,1:T(8,128)(2,1)S(1)} %collective-permute-done.2), channel_id=1, source_target_pairs={{0,2},{2,4},{4,6},{6,8},{8,10},{10,12},{12,14},{14,16},{16,18},{18... | collective-permute-start | bytes 589832 | tf_op jit(solution)/shard_map/ppermute | solution.py:17
  24.7 9.7 %collective-permute-start.10 = (bf16[512,192]{0,1:T(8,128)(2,1)S(1)}, bf16[512,192]{0,1:T(8,128)(2,1)S(1)}, u32[]{:S(2)}, u32[]{:S(2)}) collective-permute-start(bf16[512,192]{0,1:T(8,128)(2,1)S(1)} %collective-permute-done.9), channel_id=1, source_target_pairs={{0,30},{2,0},{4,2},{6,4},{8,6},{10,8},{12,10},{14,12},{16,14},{18,... | collective-permute-start | bytes 589832 | tf_op jit(solution)/shard_map/ppermute | solution.py:21
  32.6 7.8 %collective-permute-start.4 = (bf16[512,192]{0,1:T(8,128)(2,1)S(1)}, bf16[512,192]{0,1:T(8,128)(2,1)S(1)}, u32[]{:S(2)}, u32[]{:S(2)}) collective-permute-start(bf16[512,192]{0,1:T(8,128)(2,1)S(1)} %collective-permute-done.3), channel_id=1, source_target_pairs={{0,2},{2,4},{4,6},{6,8},{8,10},{10,12},{12,14},{14,16},{16,18},{18... | collective-permute-start | bytes 589832 | tf_op jit(solution)/shard_map/ppermute | solution.py:17
  34.4 13.2 %collective-permute-start.11 = (bf16[512,192]{0,1:T(8,128)(2,1)S(1)}, bf16[512,192]{0,1:T(8,128)(2,1)S(1)}, u32[]{:S(2)}, u32[]{:S(2)}) collective-permute-start(bf16[512,192]{0,1:T(8,128)(2,1)S(1)} %collective-permute-done.10), channel_id=1, source_target_pairs={{0,30},{2,0},{4,2},{6,4},{8,6},{10,8},{12,10},{14,12},{16,14},{18,... | collective-permute-start | bytes 589832 | tf_op jit(solution)/shard_map/ppermute | solution.py:21
  40.4 11.8 %collective-permute-start.5 = (bf16[512,192]{0,1:T(8,128)(2,1)S(1)}, bf16[512,192]{0,1:T(8,128)(2,1)}, u32[]{:S(2)}, u32[]{:S(2)}) collective-permute-start(bf16[512,192]{0,1:T(8,128)(2,1)S(1)} %collective-permute-done.4), channel_id=1, source_target_pairs={{0,2},{2,4},{4,6},{6,8},{8,10},{10,12},{12,14},{14,16},{16,18},{18... | collective-permute-start | bytes 589832 | tf_op jit(solution)/shard_map/ppermute | solution.py:17
  40.4 31.0 %copy-start = (bf16[512,192]{0,1:T(8,128)(2,1)S(1)}, bf16[512,192]{0,1:T(8,128)(2,1)}, u32[]{:S(2)}) copy-start(bf16[512,192]{0,1:T(8,128)(2,1)} %param.7) | copy-start | bytes 589828
  44.1 16.2 %all-to-all-start = ((bf16[2,512,512]{2,1,0:T(8,128)(2,1)}), bf16[2,512,512]{2,1,0:T(8,128)(2,1)S(1)}, u32[]{:S(2)}, u32[]{:S(2)}) async-start(bf16[2,512,512]{2,1,0:T(8,128)(2,1)} %copy.10), calls=%async_computation | async-start | bytes 2097152 | tf_op jit(solution)/shard_map/all_to_all | solution.py:35
  47.7 7.7 %collective-permute-start.12 = (bf16[512,192]{0,1:T(8,128)(2,1)S(1)}, bf16[512,192]{0,1:T(8,128)(2,1)S(1)}, u32[]{:S(2)}, u32[]{:S(2)}) collective-permute-start(bf16[512,192]{0,1:T(8,128)(2,1)S(1)} %collective-permute-done.11), channel_id=1, source_target_pairs={{0,30},{2,0},{4,2},{6,4},{8,6},{10,8},{12,10},{14,12},{16,14},{18,... | collective-permute-start | bytes 589832 | tf_op jit(solution)/shard_map/ppermute | solution.py:21
  52.2 8.1 %collective-permute-start.6 = (bf16[512,192]{0,1:T(8,128)(2,1)}, bf16[512,192]{0,1:T(8,128)(2,1)}, u32[]{:S(2)}, u32[]{:S(2)}) collective-permute-start(bf16[512,192]{0,1:T(8,128)(2,1)} %collective-permute-done.5), channel_id=1, source_target_pairs={{0,2},{2,4},{4,6},{6,8},{8,10},{10,12},{12,14},{14,16},{16,18},{18... | collective-permute-start | bytes 589832 | tf_op jit(solution)/shard_map/ppermute | solution.py:17
  55.3 7.9 %collective-permute-start.13 = (bf16[512,192]{0,1:T(8,128)(2,1)S(1)}, bf16[512,192]{0,1:T(8,128)(2,1)S(1)}, u32[]{:S(2)}, u32[]{:S(2)}) collective-permute-start(bf16[512,192]{0,1:T(8,128)(2,1)S(1)} %collective-permute-done.12), channel_id=1, source_target_pairs={{0,30},{2,0},{4,2},{6,4},{8,6},{10,8},{12,10},{14,12},{16,14},{18,... | collective-permute-start | bytes 589832 | tf_op jit(solution)/shard_map/ppermute | solution.py:21
  60.3 8.1 %collective-permute-start.7 = (bf16[512,192]{0,1:T(8,128)(2,1)}, bf16[512,192]{0,1:T(8,128)(2,1)}, u32[]{:S(2)}, u32[]{:S(2)}) collective-permute-start(bf16[512,192]{0,1:T(8,128)(2,1)} %collective-permute-done.6), channel_id=1, source_target_pairs={{0,2},{2,4},{4,6},{6,8},{8,10},{10,12},{12,14},{14,16},{16,18},{18... | collective-permute-start | bytes 589832 | tf_op jit(solution)/shard_map/ppermute | solution.py:17
  61.4 13.3 %copy-start.1 = (bf16[512,512]{1,0:T(8,128)(2,1)S(1)}, bf16[512,512]{1,0:T(8,128)(2,1)}, u32[]{:S(2)}) copy-start(bf16[512,512]{1,0:T(8,128)(2,1)} %reduce_sum.12) | copy-start | bytes 1572868
  63.2 8.3 %collective-permute-start.14 = (bf16[512,192]{0,1:T(8,128)(2,1)S(1)}, bf16[512,192]{0,1:T(8,128)(2,1)S(1)}, u32[]{:S(2)}, u32[]{:S(2)}) collective-permute-start(bf16[512,192]{0,1:T(8,128)(2,1)S(1)} %collective-permute-done.13), channel_id=1, source_target_pairs={{0,30},{2,0},{4,2},{6,4},{8,6},{10,8},{12,10},{14,12},{16,14},{18,... | collective-permute-start | bytes 589832 | tf_op jit(solution)/shard_map/ppermute | solution.py:21
